TPU v7x, 512 devices: a whole 4x4x16 slice. The times are simulated.
512 devices in a mesh: prow: 16 (over y, x), pcol: 32 (over z, core).
Axes of the slice: x: 4, y: 4, z: 16, core: 2. Of those that a mesh axis runs over, the one named last changes fastest.
Arguments:
- factor_tiles: bfloat16 [16, 1024, 1, 16, 1024], P(None, 'pcol', None, 'prow'), may hold values from -0.03125 to 0.03125
- inverse_blocks: bfloat16 [1, 16, 1024, 1024], P(None, 'prow'), may hold values from -1 to 3, as said below
- demand: bfloat16 [16, 1024, 256], P(None, 'pcol'), may hold values from -6 to 6
Outputs:
- solved: bfloat16 [1, 16, 1024, 256], P(None, 'prow')
Inputs may be any that keep to these rules, and one draw needn't show every extreme that they name: `inverse_blocks`: each [1024, 1024] block is lower triangular with a positive diagonal.
All inputs are finite; a program needn't handle non-finite values.
Results may differ from a plain program's by a relative error of at most 0.0075.
Values may be sent and summed in bfloat16 or wider, within the bound.
A program may use at most 64 MiB of HBM per device.

v0:
```python
import jax
import jax.numpy as jnp
from jax import lax
from jax.sharding import PartitionSpec as P


def on_device(factor_tiles, inverse_blocks, demand):
    block_count, slice_rows, col_slots, single, block_width = factor_tiles.shape
    columns = demand.shape[2]
    prow_size = lax.axis_size("prow")
    my_row = lax.axis_index("prow")
    row_tiles = factor_tiles.reshape(block_count, slice_rows, col_slots * block_width)
    inverse = inverse_blocks.reshape(col_slots, block_width, block_width)
    owned_blocks = jnp.zeros((col_slots, block_width, columns), jnp.bfloat16)
    pending = jnp.zeros((block_count, slice_rows, columns), jnp.float32)

    def advance(step_index, carried):
        owned_blocks, pending = carried
        owner_row = step_index % prow_size
        slot_index = step_index // prow_size
        is_owner = my_row == owner_row
        partial_sum = lax.dynamic_index_in_dim(pending, step_index, 0, keepdims=False)
        summed = lax.psum(partial_sum, "prow")
        target = lax.dynamic_index_in_dim(demand, step_index, 0, keepdims=False)
        residual = (target.astype(jnp.float32) - summed).astype(jnp.bfloat16)
        block_inv = lax.dynamic_index_in_dim(inverse, slot_index, 0, keepdims=False)
        apply_running = jnp.zeros((block_width, columns), jnp.float32)
        segment = lax.all_gather(residual, "pcol", axis=0, tiled=True)
        solved = lax.cond(
            is_owner,
            lambda: jnp.dot(block_inv, segment, preferred_element_type=jnp.float32),
            lambda: apply_running,
        ).astype(jnp.bfloat16)
        owned_blocks = jnp.where(
            is_owner,
            lax.dynamic_update_index_in_dim(owned_blocks, solved, slot_index, 0),
            owned_blocks,
        )
        pending = lax.cond(
            is_owner,
            lambda running: running
            + jnp.einsum("krw,wn->krn", row_tiles, solved, preferred_element_type=jnp.float32),
            lambda running: running,
            pending,
        )
        return (owned_blocks, pending)

    owned_blocks, pending = lax.fori_loop(0, block_count, advance, (owned_blocks, pending))
    return owned_blocks.reshape(col_slots, 1, block_width, columns)


def solution(mesh):
    placed = (
        P(None, "pcol", None, "prow", None),
        P(None, "prow", None, None),
        P(None, "pcol", None),
    )
    return jax.shard_map(
        on_device,
        mesh=mesh,
        in_specs=placed,
        out_specs=P(None, "prow", None, None),
        check_vma=False,
    )
```

profile of v0, /device:TPU:1, one launch (start us, length us, event | category | flops | bytes accessed | tf_op | source)
XLA Modules:
  0.0 1639.2 jit_solution(5200162110590774931)
XLA Ops:
  0.1 1638.4 %while.21 = (s32[]{:T(128)}, bf16[1,1024,256]{2,1,0:T(8,128)(2,1)S(1)}, f32[16,32,256]{2,1,0:T(8,128)S(1)}, s32[]{:T(128)}, bf16[16,32,256]{2,1,0:T(8,128)(2,1)}...) while((s32[]{:T(128)}, ...), condition=%wide.region_6.7_spmd.clone, body=%wide.region_0.6_spmd.clone.sunk | while | flops 806256640 | bytes 13320484 | solution.py:48
  0.1 61.6 %psum.16 = f32[32,256]{1,0:T(8,128)S(1)} all-reduce(f32[32,256]{1,0:T(8,128)S(1)} %dynamic-slice_bitcast_fusion.2), channel_id=1, replica_groups=mesh['prow'=16,'pcol'=32] {'prow'}, use_global_device_ids=true, to_apply=%region_1.1 | all-reduce | flops 8192 | bytes 65536 | tf_op jit(solution)/shard_map/while/body/eval_jaxpr/psum | solution.py:23
  62.4 52.0 %all_gather.12 = bf16[1024,256]{1,0:T(8,128)(2,1)S(1)} all-gather(bf16[32,256]{1,0:T(8,128)(2,1)S(1)} %fusion.10), channel_id=1, replica_groups=mesh['prow'=16,'pcol'=32] {'pcol'}, dimensions={0}, use_global_device_ids=true | all-gather | bytes 540672 | tf_op jit(solution)/shard_map/while/body/eval_jaxpr/all_gather | solution.py:28
  120.4 55.8 %psum.16 = f32[32,256]{1,0:T(8,128)S(1)} all-reduce(f32[32,256]{1,0:T(8,128)S(1)} %dynamic-slice_bitcast_fusion.2), channel_id=1, replica_groups=mesh['prow'=16,'pcol'=32] {'prow'}, use_global_device_ids=true, to_apply=%region_1.1 | all-reduce | flops 8192 | bytes 65536 | tf_op jit(solution)/shard_map/while/body/eval_jaxpr/psum | solution.py:23
  176.9 42.0 %all_gather.12 = bf16[1024,256]{1,0:T(8,128)(2,1)S(1)} all-gather(bf16[32,256]{1,0:T(8,128)(2,1)S(1)} %fusion.10), channel_id=1, replica_groups=mesh['prow'=16,'pcol'=32] {'pcol'}, dimensions={0}, use_global_device_ids=true | all-gather | bytes 540672 | tf_op jit(solution)/shard_map/while/body/eval_jaxpr/all_gather | solution.py:28
  220.5 58.3 %psum.16 = f32[32,256]{1,0:T(8,128)S(1)} all-reduce(f32[32,256]{1,0:T(8,128)S(1)} %dynamic-slice_bitcast_fusion.2), channel_id=1, replica_groups=mesh['prow'=16,'pcol'=32] {'prow'}, use_global_device_ids=true, to_apply=%region_1.1 | all-reduce | flops 8192 | bytes 65536 | tf_op jit(solution)/shard_map/while/body/eval_jaxpr/psum | solution.py:23
  279.5 44.1 %all_gather.12 = bf16[1024,256]{1,0:T(8,128)(2,1)S(1)} all-gather(bf16[32,256]{1,0:T(8,128)(2,1)S(1)} %fusion.10), channel_id=1, replica_groups=mesh['prow'=16,'pcol'=32] {'pcol'}, dimensions={0}, use_global_device_ids=true | all-gather | bytes 540672 | tf_op jit(solution)/shard_map/while/body/eval_jaxpr/all_gather | solution.py:28
  325.3 55.8 %psum.16 = f32[32,256]{1,0:T(8,128)S(1)} all-reduce(f32[32,256]{1,0:T(8,128)S(1)} %dynamic-slice_bitcast_fusion.2), channel_id=1, replica_groups=mesh['prow'=16,'pcol'=32] {'prow'}, use_global_device_ids=true, to_apply=%region_1.1 | all-reduce | flops 8192 | bytes 65536 | tf_op jit(solution)/shard_map/while/body/eval_jaxpr/psum | solution.py:23
  381.8 42.0 %all_gather.12 = bf16[1024,256]{1,0:T(8,128)(2,1)S(1)} all-gather(bf16[32,256]{1,0:T(8,128)(2,1)S(1)} %fusion.10), channel_id=1, replica_groups=mesh['prow'=16,'pcol'=32] {'pcol'}, dimensions={0}, use_global_device_ids=true | all-gather | bytes 540672 | tf_op jit(solution)/shard_map/while/body/eval_jaxpr/all_gather | solution.py:28
  425.4 55.8 %psum.16 = f32[32,256]{1,0:T(8,128)S(1)} all-reduce(f32[32,256]{1,0:T(8,128)S(1)} %dynamic-slice_bitcast_fusion.2), channel_id=1, replica_groups=mesh['prow'=16,'pcol'=32] {'prow'}, use_global_device_ids=true, to_apply=%region_1.1 | all-reduce | flops 8192 | bytes 65536 | tf_op jit(solution)/shard_map/while/body/eval_jaxpr/psum | solution.py:23
  481.9 43.9 %all_gather.12 = bf16[1024,256]{1,0:T(8,128)(2,1)S(1)} all-gather(bf16[32,256]{1,0:T(8,128)(2,1)S(1)} %fusion.10), channel_id=1, replica_groups=mesh['prow'=16,'pcol'=32] {'pcol'}, dimensions={0}, use_global_device_ids=true | all-gather | bytes 540672 | tf_op jit(solution)/shard_map/while/body/eval_jaxpr/all_gather | solution.py:28
  527.5 55.8 %psum.16 = f32[32,256]{1,0:T(8,128)S(1)} all-reduce(f32[32,256]{1,0:T(8,128)S(1)} %dynamic-slice_bitcast_fusion.2), channel_id=1, replica_groups=mesh['prow'=16,'pcol'=32] {'prow'}, use_global_device_ids=true, to_apply=%region_1.1 | all-reduce | flops 8192 | bytes 65536 | tf_op jit(solution)/shard_map/while/body/eval_jaxpr/psum | solution.py:23
  584.0 42.0 %all_gather.12 = bf16[1024,256]{1,0:T(8,128)(2,1)S(1)} all-gather(bf16[32,256]{1,0:T(8,128)(2,1)S(1)} %fusion.10), channel_id=1, replica_groups=mesh['prow'=16,'pcol'=32] {'pcol'}, dimensions={0}, use_global_device_ids=true | all-gather | bytes 540672 | tf_op jit(solution)/shard_map/while/body/eval_jaxpr/all_gather | solution.py:28
  627.6 55.8 %psum.16 = f32[32,256]{1,0:T(8,128)S(1)} all-reduce(f32[32,256]{1,0:T(8,128)S(1)} %dynamic-slice_bitcast_fusion.2), channel_id=1, replica_groups=mesh['prow'=16,'pcol'=32] {'prow'}, use_global_device_ids=true, to_apply=%region_1.1 | all-reduce | flops 8192 | bytes 65536 | tf_op jit(solution)/shard_map/while/body/eval_jaxpr/psum | solution.py:23
  684.1 43.9 %all_gather.12 = bf16[1024,256]{1,0:T(8,128)(2,1)S(1)} all-gather(bf16[32,256]{1,0:T(8,128)(2,1)S(1)} %fusion.10), channel_id=1, replica_groups=mesh['prow'=16,'pcol'=32] {'pcol'}, dimensions={0}, use_global_device_ids=true | all-gather | bytes 540672 | tf_op jit(solution)/shard_map/while/body/eval_jaxpr/all_gather | solution.py:28
  729.7 55.8 %psum.16 = f32[32,256]{1,0:T(8,128)S(1)} all-reduce(f32[32,256]{1,0:T(8,128)S(1)} %dynamic-slice_bitcast_fusion.2), channel_id=1, replica_groups=mesh['prow'=16,'pcol'=32] {'prow'}, use_global_device_ids=true, to_apply=%region_1.1 | all-reduce | flops 8192 | bytes 65536 | tf_op jit(solution)/shard_map/while/body/eval_jaxpr/psum | solution.py:23
  786.1 42.0 %all_gather.12 = bf16[1024,256]{1,0:T(8,128)(2,1)S(1)} all-gather(bf16[32,256]{1,0:T(8,128)(2,1)S(1)} %fusion.10), channel_id=1, replica_groups=mesh['prow'=16,'pcol'=32] {'pcol'}, dimensions={0}, use_global_device_ids=true | all-gather | bytes 540672 | tf_op jit(solution)/shard_map/while/body/eval_jaxpr/all_gather | solution.py:28
  829.8 55.8 %psum.16 = f32[32,256]{1,0:T(8,128)S(1)} all-reduce(f32[32,256]{1,0:T(8,128)S(1)} %dynamic-slice_bitcast_fusion.2), channel_id=1, replica_groups=mesh['prow'=16,'pcol'=32] {'prow'}, use_global_device_ids=true, to_apply=%region_1.1 | all-reduce | flops 8192 | bytes 65536 | tf_op jit(solution)/shard_map/while/body/eval_jaxpr/psum | solution.py:23
  886.3 43.9 %all_gather.12 = bf16[1024,256]{1,0:T(8,128)(2,1)S(1)} all-gather(bf16[32,256]{1,0:T(8,128)(2,1)S(1)} %fusion.10), channel_id=1, replica_groups=mesh['prow'=16,'pcol'=32] {'pcol'}, dimensions={0}, use_global_device_ids=true | all-gather | bytes 540672 | tf_op jit(solution)/shard_map/while/body/eval_jaxpr/all_gather | solution.py:28
  931.8 55.8 %psum.16 = f32[32,256]{1,0:T(8,128)S(1)} all-reduce(f32[32,256]{1,0:T(8,128)S(1)} %dynamic-slice_bitcast_fusion.2), channel_id=1, replica_groups=mesh['prow'=16,'pcol'=32] {'prow'}, use_global_device_ids=true, to_apply=%region_1.1 | all-reduce | flops 8192 | bytes 65536 | tf_op jit(solution)/shard_map/while/body/eval_jaxpr/psum | solution.py:23
  988.3 42.0 %all_gather.12 = bf16[1024,256]{1,0:T(8,128)(2,1)S(1)} all-gather(bf16[32,256]{1,0:T(8,128)(2,1)S(1)} %fusion.10), channel_id=1, replica_groups=mesh['prow'=16,'pcol'=32] {'pcol'}, dimensions={0}, use_global_device_ids=true | all-gather | bytes 540672 | tf_op jit(solution)/shard_map/while/body/eval_jaxpr/all_gather | solution.py:28
  1031.9 55.8 %psum.16 = f32[32,256]{1,0:T(8,128)S(1)} all-reduce(f32[32,256]{1,0:T(8,128)S(1)} %dynamic-slice_bitcast_fusion.2), channel_id=1, replica_groups=mesh['prow'=16,'pcol'=32] {'prow'}, use_global_device_ids=true, to_apply=%region_1.1 | all-reduce | flops 8192 | bytes 65536 | tf_op jit(solution)/shard_map/while/body/eval_jaxpr/psum | solution.py:23
  1088.4 43.9 %all_gather.12 = bf16[1024,256]{1,0:T(8,128)(2,1)S(1)} all-gather(bf16[32,256]{1,0:T(8,128)(2,1)S(1)} %fusion.10), channel_id=1, replica_groups=mesh['prow'=16,'pcol'=32] {'pcol'}, dimensions={0}, use_global_device_ids=true | all-gather | bytes 540672 | tf_op jit(solution)/shard_map/while/body/eval_jaxpr/all_gather | solution.py:28
  1134.0 55.8 %psum.16 = f32[32,256]{1,0:T(8,128)S(1)} all-reduce(f32[32,256]{1,0:T(8,128)S(1)} %dynamic-slice_bitcast_fusion.2), channel_id=1, replica_groups=mesh['prow'=16,'pcol'=32] {'prow'}, use_global_device_ids=true, to_apply=%region_1.1 | all-reduce | flops 8192 | bytes 65536 | tf_op jit(solution)/shard_map/while/body/eval_jaxpr/psum | solution.py:23
  1190.5 42.0 %all_gather.12 = bf16[1024,256]{1,0:T(8,128)(2,1)S(1)} all-gather(bf16[32,256]{1,0:T(8,128)(2,1)S(1)} %fusion.10), channel_id=1, replica_groups=mesh['prow'=16,'pcol'=32] {'pcol'}, dimensions={0}, use_global_device_ids=true | all-gather | bytes 540672 | tf_op jit(solution)/shard_map/while/body/eval_jaxpr/all_gather | solution.py:28
  1234.1 55.8 %psum.16 = f32[32,256]{1,0:T(8,128)S(1)} all-reduce(f32[32,256]{1,0:T(8,128)S(1)} %dynamic-slice_bitcast_fusion.2), channel_id=1, replica_groups=mesh['prow'=16,'pcol'=32] {'prow'}, use_global_device_ids=true, to_apply=%region_1.1 | all-reduce | flops 8192 | bytes 65536 | tf_op jit(solution)/shard_map/while/body/eval_jaxpr/psum | solution.py:23
  1290.6 43.9 %all_gather.12 = bf16[1024,256]{1,0:T(8,128)(2,1)S(1)} all-gather(bf16[32,256]{1,0:T(8,128)(2,1)S(1)} %fusion.10), channel_id=1, replica_groups=mesh['prow'=16,'pcol'=32] {'pcol'}, dimensions={0}, use_global_device_ids=true | all-gather | bytes 540672 | tf_op jit(solution)/shard_map/while/body/eval_jaxpr/all_gather | solution.py:28
  1336.2 55.8 %psum.16 = f32[32,256]{1,0:T(8,128)S(1)} all-reduce(f32[32,256]{1,0:T(8,128)S(1)} %dynamic-slice_bitcast_fusion.2), channel_id=1, replica_groups=mesh['prow'=16,'pcol'=32] {'prow'}, use_global_device_ids=true, to_apply=%region_1.1 | all-reduce | flops 8192 | bytes 65536 | tf_op jit(solution)/shard_map/while/body/eval_jaxpr/psum | solution.py:23
  1392.7 42.0 %all_gather.12 = bf16[1024,256]{1,0:T(8,128)(2,1)S(1)} all-gather(bf16[32,256]{1,0:T(8,128)(2,1)S(1)} %fusion.10), channel_id=1, replica_groups=mesh['prow'=16,'pcol'=32] {'pcol'}, dimensions={0}, use_global_device_ids=true | all-gather | bytes 540672 | tf_op jit(solution)/shard_map/while/body/eval_jaxpr/all_gather | solution.py:28
  1436.3 55.8 %psum.16 = f32[32,256]{1,0:T(8,128)S(1)} all-reduce(f32[32,256]{1,0:T(8,128)S(1)} %dynamic-slice_bitcast_fusion.2), channel_id=1, replica_groups=mesh['prow'=16,'pcol'=32] {'prow'}, use_global_device_ids=true, to_apply=%region_1.1 | all-reduce | flops 8192 | bytes 65536 | tf_op jit(solution)/shard_map/while/body/eval_jaxpr/psum | solution.py:23
  1492.8 43.9 %all_gather.12 = bf16[1024,256]{1,0:T(8,128)(2,1)S(1)} all-gather(bf16[32,256]{1,0:T(8,128)(2,1)S(1)} %fusion.10), channel_id=1, replica_groups=mesh['prow'=16,'pcol'=32] {'pcol'}, dimensions={0}, use_global_device_ids=true | all-gather | bytes 540672 | tf_op jit(solution)/shard_map/while/body/eval_jaxpr/all_gather | solution.py:28
  1538.4 55.8 %psum.16 = f32[32,256]{1,0:T(8,128)S(1)} all-reduce(f32[32,256]{1,0:T(8,128)S(1)} %dynamic-slice_bitcast_fusion.2), channel_id=1, replica_groups=mesh['prow'=16,'pcol'=32] {'prow'}, use_global_device_ids=true, to_apply=%region_1.1 | all-reduce | flops 8192 | bytes 65536 | tf_op jit(solution)/shard_map/while/body/eval_jaxpr/psum | solution.py:23
  (150 shorter events, 103.3 us)
Async XLA Ops:
  114.4 4.2 copy-start
  218.8 1.4 copy-start
  323.6 1.4 copy-start
  423.8 1.4 copy-start
  525.8 1.4 copy-start
  625.9 1.4 copy-start
  728.0 1.4 copy-start
  828.1 1.4 copy-start
  930.2 1.4 copy-start
  1030.3 1.4 copy-start
  1132.3 1.4 copy-start
  1232.5 1.4 copy-start
  1334.5 1.4 copy-start
  1434.6 1.4 copy-start
  1536.7 1.4 copy-start
  1636.8 1.4 copy-start
  1638.4 0.8 copy-start.1
where the time goes:
time: 1640 us
  blocking collectives  1600 us (98%)
  local copies, waits for them, and re-layouts  23 us (1%)
    psum x16, blocking collectives, advance(): summed = lax.psum(partial_sum, 'prow')  901 us
    all_gather x16, blocking collectives, advance(): segment = lax.all_gather(residual, 'pcol', axis=0, tiled=True)  695 us

commit v1 on v0

--- a/solution.py
+++ b/solution.py
@@ -1,7 +1,21 @@
+import functools
 import jax
 import jax.numpy as jnp
 from jax import lax
 from jax.sharding import PartitionSpec as P
+
+
+def name_files_over_axis(field_in, axis_no):
+    main = jnp.concatenate(
+        lax.all_to_all(
+            jnp.stack(tuple((field_in for _ in range(lax.axis_size("pcol"))))), "pcol", 0, 0
+        ),
+        axis_no,
+    )
+    return main
+
+
+sample_spread = functools.partial(name_files_over_axis, axis_no=0)
 
 
 def on_device(factor_tiles, inverse_blocks, demand):
@@ -25,7 +39,7 @@
         residual = (target.astype(jnp.float32) - summed).astype(jnp.bfloat16)
         block_inv = lax.dynamic_index_in_dim(inverse, slot_index, 0, keepdims=False)
         apply_running = jnp.zeros((block_width, columns), jnp.float32)
-        segment = lax.all_gather(residual, "pcol", axis=0, tiled=True)
+        segment = sample_spread(residual)
         solved = lax.cond(
             is_owner,
             lambda: jnp.dot(block_inv, segment, preferred_element_type=jnp.float32),

time: 1640 us -> 1800 us (1.098)
  blocking collectives: 1600 us -> 899 us
  waiting for transfers between devices: 0 us -> 536 us
  starting transfers between devices: 0 us -> 303 us
    all_gather x16 -> x0, blocking collectives: 695 us -> none  [advance(): segment = lax.all_gather(residual, 'pcol', axis=0, tiled=True)]
    all_to_all x0 -> x16, waiting for transfers between devices: none -> 536 us  [name_files_over_axis(): lax.all_to_all(jnp.stack(tuple((field_in for _ in range(lax.axis_size('pc...]
    all_to_all x0 -> x16, starting transfers between devices: none -> 303 us  [name_files_over_axis(): lax.all_to_all(jnp.stack(tuple((field_in for _ in range(lax.axis_size('pc...]
  transfers between devices with their start and end apart: 0 -> 16, of which waited for: 0 -> 16; matrix products, arithmetic and copies ran while one was open for 0% -> 0% of each run, Pallas kernels for 0% -> 0%
where the time goes in v1:
time: 1800 us
  blocking collectives  899 us (50%)
  waiting for transfers between devices  536 us (30%)
  starting transfers between devices  303 us (17%)
  local copies, waits for them, and re-layouts  36.7 us (2%)
    psum x16, blocking collectives, advance(): summed = lax.psum(partial_sum, 'prow')  899 us
    all_to_all x16, waiting for transfers between devices, name_files_over_axis(): lax.all_to_all(jnp.stack(tuple((field_in for _ in range(lax.axis_size('pc...  536 us
    all_to_all x16, starting transfers between devices, name_files_over_axis(): lax.all_to_all(jnp.stack(tuple((field_in for _ in range(lax.axis_size('pc...  303 us
  transfers between devices with their start and end apart: 16, of which 16 were waited for; matrix products, arithmetic and copies ran while one was open for 0% of the time, Pallas kernels for 0%

profile of v1, /device:TPU:1, one launch (start us, length us, event | category | flops | bytes accessed | tf_op | source)
XLA Modules:
  0.0 1795.4 jit_solution(15111454151850758994)
XLA Ops:
  0.1 1794.6 %while.21 = (s32[]{:T(128)}, bf16[1,1024,256]{2,1,0:T(8,128)(2,1)S(1)}, f32[16,32,256]{2,1,0:T(8,128)S(1)}, s32[]{:T(128)}, bf16[16,32,256]{2,1,0:T(8,128)(2,1)}...) while((s32[]{:T(128)}, ...), condition=%wide.region_6.7_spmd.clone, body=%wide.region_0.6_spmd.clone.sunk | while | flops 806256640 | bytes 14893380 | solution.py:62
  0.1 61.6 %psum.16 = f32[32,256]{1,0:T(8,128)S(1)} all-reduce(f32[32,256]{1,0:T(8,128)S(1)} %dynamic-slice_bitcast_fusion.2), channel_id=1, replica_groups=mesh['prow'=16,'pcol'=32] {'prow'}, use_global_device_ids=true, to_apply=%region_1.1 | all-reduce | flops 8192 | bytes 65536 | tf_op jit(solution)/shard_map/while/body/eval_jaxpr/psum | solution.py:37
  132.5 56.1 %psum.16 = f32[32,256]{1,0:T(8,128)S(1)} all-reduce(f32[32,256]{1,0:T(8,128)S(1)} %dynamic-slice_bitcast_fusion.2), channel_id=1, replica_groups=mesh['prow'=16,'pcol'=32] {'prow'}, use_global_device_ids=true, to_apply=%region_1.1 | all-reduce | flops 8192 | bytes 65536 | tf_op jit(solution)/shard_map/while/body/eval_jaxpr/psum | solution.py:37
  207.7 33.5 %all-to-all-done = bf16[32,32,256]{2,1,0:T(8,128)(2,1)S(1)} async-done(((bf16[32,32,256]{2,1,0:T(8,128)(2,1)}), bf16[32,32,256]{2,1,0:T(8,128)(2,1)S(1)}, u32[]{:S(2)}, u32[]{:S(2)}) %all-to-all-start) | async-done | bytes 524320 | tf_op jit(solution)/shard_map/while/body/eval_jaxpr/all_to_all | solution.py:10
  242.9 58.1 %psum.16 = f32[32,256]{1,0:T(8,128)S(1)} all-reduce(f32[32,256]{1,0:T(8,128)S(1)} %dynamic-slice_bitcast_fusion.2), channel_id=1, replica_groups=mesh['prow'=16,'pcol'=32] {'prow'}, use_global_device_ids=true, to_apply=%region_1.1 | all-reduce | flops 8192 | bytes 65536 | tf_op jit(solution)/shard_map/while/body/eval_jaxpr/psum | solution.py:37
  321.1 33.5 %all-to-all-done = bf16[32,32,256]{2,1,0:T(8,128)(2,1)S(1)} async-done(((bf16[32,32,256]{2,1,0:T(8,128)(2,1)}), bf16[32,32,256]{2,1,0:T(8,128)(2,1)S(1)}, u32[]{:S(2)}, u32[]{:S(2)}) %all-to-all-start) | async-done | bytes 524320 | tf_op jit(solution)/shard_map/while/body/eval_jaxpr/all_to_all | solution.py:10
  356.3 55.6 %psum.16 = f32[32,256]{1,0:T(8,128)S(1)} all-reduce(f32[32,256]{1,0:T(8,128)S(1)} %dynamic-slice_bitcast_fusion.2), channel_id=1, replica_groups=mesh['prow'=16,'pcol'=32] {'prow'}, use_global_device_ids=true, to_apply=%region_1.1 | all-reduce | flops 8192 | bytes 65536 | tf_op jit(solution)/shard_map/while/body/eval_jaxpr/psum | solution.py:37
  431.7 33.5 %all-to-all-done = bf16[32,32,256]{2,1,0:T(8,128)(2,1)S(1)} async-done(((bf16[32,32,256]{2,1,0:T(8,128)(2,1)}), bf16[32,32,256]{2,1,0:T(8,128)(2,1)S(1)}, u32[]{:S(2)}, u32[]{:S(2)}) %all-to-all-start) | async-done | bytes 524320 | tf_op jit(solution)/shard_map/while/body/eval_jaxpr/all_to_all | solution.py:10
  466.9 55.6 %psum.16 = f32[32,256]{1,0:T(8,128)S(1)} all-reduce(f32[32,256]{1,0:T(8,128)S(1)} %dynamic-slice_bitcast_fusion.2), channel_id=1, replica_groups=mesh['prow'=16,'pcol'=32] {'prow'}, use_global_device_ids=true, to_apply=%region_1.1 | all-reduce | flops 8192 | bytes 65536 | tf_op jit(solution)/shard_map/while/body/eval_jaxpr/psum | solution.py:37
  542.4 33.5 %all-to-all-done = bf16[32,32,256]{2,1,0:T(8,128)(2,1)S(1)} async-done(((bf16[32,32,256]{2,1,0:T(8,128)(2,1)}), bf16[32,32,256]{2,1,0:T(8,128)(2,1)S(1)}, u32[]{:S(2)}, u32[]{:S(2)}) %all-to-all-start) | async-done | bytes 524320 | tf_op jit(solution)/shard_map/while/body/eval_jaxpr/all_to_all | solution.py:10
  577.5 55.6 %psum.16 = f32[32,256]{1,0:T(8,128)S(1)} all-reduce(f32[32,256]{1,0:T(8,128)S(1)} %dynamic-slice_bitcast_fusion.2), channel_id=1, replica_groups=mesh['prow'=16,'pcol'=32] {'prow'}, use_global_device_ids=true, to_apply=%region_1.1 | all-reduce | flops 8192 | bytes 65536 | tf_op jit(solution)/shard_map/while/body/eval_jaxpr/psum | solution.py:37
  653.0 33.5 %all-to-all-done = bf16[32,32,256]{2,1,0:T(8,128)(2,1)S(1)} async-done(((bf16[32,32,256]{2,1,0:T(8,128)(2,1)}), bf16[32,32,256]{2,1,0:T(8,128)(2,1)S(1)}, u32[]{:S(2)}, u32[]{:S(2)}) %all-to-all-start) | async-done | bytes 524320 | tf_op jit(solution)/shard_map/while/body/eval_jaxpr/all_to_all | solution.py:10
  688.2 55.6 %psum.16 = f32[32,256]{1,0:T(8,128)S(1)} all-reduce(f32[32,256]{1,0:T(8,128)S(1)} %dynamic-slice_bitcast_fusion.2), channel_id=1, replica_groups=mesh['prow'=16,'pcol'=32] {'prow'}, use_global_device_ids=true, to_apply=%region_1.1 | all-reduce | flops 8192 | bytes 65536 | tf_op jit(solution)/shard_map/while/body/eval_jaxpr/psum | solution.py:37
  763.7 33.5 %all-to-all-done = bf16[32,32,256]{2,1,0:T(8,128)(2,1)S(1)} async-done(((bf16[32,32,256]{2,1,0:T(8,128)(2,1)}), bf16[32,32,256]{2,1,0:T(8,128)(2,1)S(1)}, u32[]{:S(2)}, u32[]{:S(2)}) %all-to-all-start) | async-done | bytes 524320 | tf_op jit(solution)/shard_map/while/body/eval_jaxpr/all_to_all | solution.py:10
  798.8 55.6 %psum.16 = f32[32,256]{1,0:T(8,128)S(1)} all-reduce(f32[32,256]{1,0:T(8,128)S(1)} %dynamic-slice_bitcast_fusion.2), channel_id=1, replica_groups=mesh['prow'=16,'pcol'=32] {'prow'}, use_global_device_ids=true, to_apply=%region_1.1 | all-reduce | flops 8192 | bytes 65536 | tf_op jit(solution)/shard_map/while/body/eval_jaxpr/psum | solution.py:37
  874.3 33.5 %all-to-all-done = bf16[32,32,256]{2,1,0:T(8,128)(2,1)S(1)} async-done(((bf16[32,32,256]{2,1,0:T(8,128)(2,1)}), bf16[32,32,256]{2,1,0:T(8,128)(2,1)S(1)}, u32[]{:S(2)}, u32[]{:S(2)}) %all-to-all-start) | async-done | bytes 524320 | tf_op jit(solution)/shard_map/while/body/eval_jaxpr/all_to_all | solution.py:10
  909.5 55.6 %psum.16 = f32[32,256]{1,0:T(8,128)S(1)} all-reduce(f32[32,256]{1,0:T(8,128)S(1)} %dynamic-slice_bitcast_fusion.2), channel_id=1, replica_groups=mesh['prow'=16,'pcol'=32] {'prow'}, use_global_device_ids=true, to_apply=%region_1.1 | all-reduce | flops 8192 | bytes 65536 | tf_op jit(solution)/shard_map/while/body/eval_jaxpr/psum | solution.py:37
  985.0 33.5 %all-to-all-done = bf16[32,32,256]{2,1,0:T(8,128)(2,1)S(1)} async-done(((bf16[32,32,256]{2,1,0:T(8,128)(2,1)}), bf16[32,32,256]{2,1,0:T(8,128)(2,1)S(1)}, u32[]{:S(2)}, u32[]{:S(2)}) %all-to-all-start) | async-done | bytes 524320 | tf_op jit(solution)/shard_map/while/body/eval_jaxpr/all_to_all | solution.py:10
  1020.1 55.6 %psum.16 = f32[32,256]{1,0:T(8,128)S(1)} all-reduce(f32[32,256]{1,0:T(8,128)S(1)} %dynamic-slice_bitcast_fusion.2), channel_id=1, replica_groups=mesh['prow'=16,'pcol'=32] {'prow'}, use_global_device_ids=true, to_apply=%region_1.1 | all-reduce | flops 8192 | bytes 65536 | tf_op jit(solution)/shard_map/while/body/eval_jaxpr/psum | solution.py:37
  1095.6 33.5 %all-to-all-done = bf16[32,32,256]{2,1,0:T(8,128)(2,1)S(1)} async-done(((bf16[32,32,256]{2,1,0:T(8,128)(2,1)}), bf16[32,32,256]{2,1,0:T(8,128)(2,1)S(1)}, u32[]{:S(2)}, u32[]{:S(2)}) %all-to-all-start) | async-done | bytes 524320 | tf_op jit(solution)/shard_map/while/body/eval_jaxpr/all_to_all | solution.py:10
  1130.8 55.6 %psum.16 = f32[32,256]{1,0:T(8,128)S(1)} all-reduce(f32[32,256]{1,0:T(8,128)S(1)} %dynamic-slice_bitcast_fusion.2), channel_id=1, replica_groups=mesh['prow'=16,'pcol'=32] {'prow'}, use_global_device_ids=true, to_apply=%region_1.1 | all-reduce | flops 8192 | bytes 65536 | tf_op jit(solution)/shard_map/while/body/eval_jaxpr/psum | solution.py:37
  1206.3 33.5 %all-to-all-done = bf16[32,32,256]{2,1,0:T(8,128)(2,1)S(1)} async-done(((bf16[32,32,256]{2,1,0:T(8,128)(2,1)}), bf16[32,32,256]{2,1,0:T(8,128)(2,1)S(1)}, u32[]{:S(2)}, u32[]{:S(2)}) %all-to-all-start) | async-done | bytes 524320 | tf_op jit(solution)/shard_map/while/body/eval_jaxpr/all_to_all | solution.py:10
  1241.4 55.6 %psum.16 = f32[32,256]{1,0:T(8,128)S(1)} all-reduce(f32[32,256]{1,0:T(8,128)S(1)} %dynamic-slice_bitcast_fusion.2), channel_id=1, replica_groups=mesh['prow'=16,'pcol'=32] {'prow'}, use_global_device_ids=true, to_apply=%region_1.1 | all-reduce | flops 8192 | bytes 65536 | tf_op jit(solution)/shard_map/while/body/eval_jaxpr/psum | solution.py:37
  1316.9 33.5 %all-to-all-done = bf16[32,32,256]{2,1,0:T(8,128)(2,1)S(1)} async-done(((bf16[32,32,256]{2,1,0:T(8,128)(2,1)}), bf16[32,32,256]{2,1,0:T(8,128)(2,1)S(1)}, u32[]{:S(2)}, u32[]{:S(2)}) %all-to-all-start) | async-done | bytes 524320 | tf_op jit(solution)/shard_map/while/body/eval_jaxpr/all_to_all | solution.py:10
  1352.1 55.6 %psum.16 = f32[32,256]{1,0:T(8,128)S(1)} all-reduce(f32[32,256]{1,0:T(8,128)S(1)} %dynamic-slice_bitcast_fusion.2), channel_id=1, replica_groups=mesh['prow'=16,'pcol'=32] {'prow'}, use_global_device_ids=true, to_apply=%region_1.1 | all-reduce | flops 8192 | bytes 65536 | tf_op jit(solution)/shard_map/while/body/eval_jaxpr/psum | solution.py:37
  1427.5 33.5 %all-to-all-done = bf16[32,32,256]{2,1,0:T(8,128)(2,1)S(1)} async-done(((bf16[32,32,256]{2,1,0:T(8,128)(2,1)}), bf16[32,32,256]{2,1,0:T(8,128)(2,1)S(1)}, u32[]{:S(2)}, u32[]{:S(2)}) %all-to-all-start) | async-done | bytes 524320 | tf_op jit(solution)/shard_map/while/body/eval_jaxpr/all_to_all | solution.py:10
  1462.7 55.6 %psum.16 = f32[32,256]{1,0:T(8,128)S(1)} all-reduce(f32[32,256]{1,0:T(8,128)S(1)} %dynamic-slice_bitcast_fusion.2), channel_id=1, replica_groups=mesh['prow'=16,'pcol'=32] {'prow'}, use_global_device_ids=true, to_apply=%region_1.1 | all-reduce | flops 8192 | bytes 65536 | tf_op jit(solution)/shard_map/while/body/eval_jaxpr/psum | solution.py:37
  1538.2 33.5 %all-to-all-done = bf16[32,32,256]{2,1,0:T(8,128)(2,1)S(1)} async-done(((bf16[32,32,256]{2,1,0:T(8,128)(2,1)}), bf16[32,32,256]{2,1,0:T(8,128)(2,1)S(1)}, u32[]{:S(2)}, u32[]{:S(2)}) %all-to-all-start) | async-done | bytes 524320 | tf_op jit(solution)/shard_map/while/body/eval_jaxpr/all_to_all | solution.py:10
  1573.4 55.6 %psum.16 = f32[32,256]{1,0:T(8,128)S(1)} all-reduce(f32[32,256]{1,0:T(8,128)S(1)} %dynamic-slice_bitcast_fusion.2), channel_id=1, replica_groups=mesh['prow'=16,'pcol'=32] {'prow'}, use_global_device_ids=true, to_apply=%region_1.1 | all-reduce | flops 8192 | bytes 65536 | tf_op jit(solution)/shard_map/while/body/eval_jaxpr/psum | solution.py:37
  1648.8 33.5 %all-to-all-done = bf16[32,32,256]{2,1,0:T(8,128)(2,1)S(1)} async-done(((bf16[32,32,256]{2,1,0:T(8,128)(2,1)}), bf16[32,32,256]{2,1,0:T(8,128)(2,1)S(1)}, u32[]{:S(2)}, u32[]{:S(2)}) %all-to-all-start) | async-done | bytes 524320 | tf_op jit(solution)/shard_map/while/body/eval_jaxpr/all_to_all | solution.py:10
  1684.0 55.6 %psum.16 = f32[32,256]{1,0:T(8,128)S(1)} all-reduce(f32[32,256]{1,0:T(8,128)S(1)} %dynamic-slice_bitcast_fusion.2), channel_id=1, replica_groups=mesh['prow'=16,'pcol'=32] {'prow'}, use_global_device_ids=true, to_apply=%region_1.1 | all-reduce | flops 8192 | bytes 65536 | tf_op jit(solution)/shard_map/while/body/eval_jaxpr/psum | solution.py:37
  1759.5 33.5 %all-to-all-done = bf16[32,32,256]{2,1,0:T(8,128)(2,1)S(1)} async-done(((bf16[32,32,256]{2,1,0:T(8,128)(2,1)}), bf16[32,32,256]{2,1,0:T(8,128)(2,1)S(1)}, u32[]{:S(2)}, u32[]{:S(2)}) %all-to-all-start) | async-done | bytes 524320 | tf_op jit(solution)/shard_map/while/body/eval_jaxpr/all_to_all | solution.py:10
  (182 shorter events, 411.5 us)
Async XLA Ops:
  63.2 63.3 %all-to-all-start = ((bf16[32,32,256]{2,1,0:T(8,128)(2,1)}), bf16[32,32,256]{2,1,0:T(8,128)(2,1)S(1)}, u32[]{:S(2)}, u32[]{:S(2)}) async-start(bf16[32,32,256]{2,1,0:T(8,128)(2,1)} %stack.8), calls=%async_computation | async-start | bytes 1048576 | tf_op jit(solution)/shard_map/while/body/eval_jaxpr/all_to_all | solution.py:10
  126.5 4.2 copy-start
  190.2 51.0 %all-to-all-start = ((bf16[32,32,256]{2,1,0:T(8,128)(2,1)}), bf16[32,32,256]{2,1,0:T(8,128)(2,1)S(1)}, u32[]{:S(2)}, u32[]{:S(2)}) async-start(bf16[32,32,256]{2,1,0:T(8,128)(2,1)} %stack.8), calls=%async_computation | async-start | bytes 1048576 | tf_op jit(solution)/shard_map/while/body/eval_jaxpr/all_to_all | solution.py:10
  241.2 1.4 copy-start
  302.5 52.1 %all-to-all-start = ((bf16[32,32,256]{2,1,0:T(8,128)(2,1)}), bf16[32,32,256]{2,1,0:T(8,128)(2,1)S(1)}, u32[]{:S(2)}, u32[]{:S(2)}) async-start(bf16[32,32,256]{2,1,0:T(8,128)(2,1)} %stack.8), calls=%async_computation | async-start | bytes 1048576 | tf_op jit(solution)/shard_map/while/body/eval_jaxpr/all_to_all | solution.py:10
  354.6 1.4 copy-start
  413.5 51.8 %all-to-all-start = ((bf16[32,32,256]{2,1,0:T(8,128)(2,1)}), bf16[32,32,256]{2,1,0:T(8,128)(2,1)S(1)}, u32[]{:S(2)}, u32[]{:S(2)}) async-start(bf16[32,32,256]{2,1,0:T(8,128)(2,1)} %stack.8), calls=%async_computation | async-start | bytes 1048576 | tf_op jit(solution)/shard_map/while/body/eval_jaxpr/all_to_all | solution.py:10
  465.2 1.4 copy-start
  524.1 51.8 %all-to-all-start = ((bf16[32,32,256]{2,1,0:T(8,128)(2,1)}), bf16[32,32,256]{2,1,0:T(8,128)(2,1)S(1)}, u32[]{:S(2)}, u32[]{:S(2)}) async-start(bf16[32,32,256]{2,1,0:T(8,128)(2,1)} %stack.8), calls=%async_computation | async-start | bytes 1048576 | tf_op jit(solution)/shard_map/while/body/eval_jaxpr/all_to_all | solution.py:10
  575.9 1.4 copy-start
  634.8 51.8 %all-to-all-start = ((bf16[32,32,256]{2,1,0:T(8,128)(2,1)}), bf16[32,32,256]{2,1,0:T(8,128)(2,1)S(1)}, u32[]{:S(2)}, u32[]{:S(2)}) async-start(bf16[32,32,256]{2,1,0:T(8,128)(2,1)} %stack.8), calls=%async_computation | async-start | bytes 1048576 | tf_op jit(solution)/shard_map/while/body/eval_jaxpr/all_to_all | solution.py:10
  686.5 1.4 copy-start
  745.4 51.8 %all-to-all-start = ((bf16[32,32,256]{2,1,0:T(8,128)(2,1)}), bf16[32,32,256]{2,1,0:T(8,128)(2,1)S(1)}, u32[]{:S(2)}, u32[]{:S(2)}) async-start(bf16[32,32,256]{2,1,0:T(8,128)(2,1)} %stack.8), calls=%async_computation | async-start | bytes 1048576 | tf_op jit(solution)/shard_map/while/body/eval_jaxpr/all_to_all | solution.py:10
  797.2 1.4 copy-start
  856.0 51.8 %all-to-all-start = ((bf16[32,32,256]{2,1,0:T(8,128)(2,1)}), bf16[32,32,256]{2,1,0:T(8,128)(2,1)S(1)}, u32[]{:S(2)}, u32[]{:S(2)}) async-start(bf16[32,32,256]{2,1,0:T(8,128)(2,1)} %stack.8), calls=%async_computation | async-start | bytes 1048576 | tf_op jit(solution)/shard_map/while/body/eval_jaxpr/all_to_all | solution.py:10
  907.8 1.4 copy-start
  966.7 51.8 %all-to-all-start = ((bf16[32,32,256]{2,1,0:T(8,128)(2,1)}), bf16[32,32,256]{2,1,0:T(8,128)(2,1)S(1)}, u32[]{:S(2)}, u32[]{:S(2)}) async-start(bf16[32,32,256]{2,1,0:T(8,128)(2,1)} %stack.8), calls=%async_computation | async-start | bytes 1048576 | tf_op jit(solution)/shard_map/while/body/eval_jaxpr/all_to_all | solution.py:10
  1018.5 1.4 copy-start
  1077.3 51.8 %all-to-all-start = ((bf16[32,32,256]{2,1,0:T(8,128)(2,1)}), bf16[32,32,256]{2,1,0:T(8,128)(2,1)S(1)}, u32[]{:S(2)}, u32[]{:S(2)}) async-start(bf16[32,32,256]{2,1,0:T(8,128)(2,1)} %stack.8), calls=%async_computation | async-start | bytes 1048576 | tf_op jit(solution)/shard_map/while/body/eval_jaxpr/all_to_all | solution.py:10
  1129.1 1.4 copy-start
  1188.0 51.8 %all-to-all-start = ((bf16[32,32,256]{2,1,0:T(8,128)(2,1)}), bf16[32,32,256]{2,1,0:T(8,128)(2,1)S(1)}, u32[]{:S(2)}, u32[]{:S(2)}) async-start(bf16[32,32,256]{2,1,0:T(8,128)(2,1)} %stack.8), calls=%async_computation | async-start | bytes 1048576 | tf_op jit(solution)/shard_map/while/body/eval_jaxpr/all_to_all | solution.py:10
  1239.8 1.4 copy-start
  1298.6 51.8 %all-to-all-start = ((bf16[32,32,256]{2,1,0:T(8,128)(2,1)}), bf16[32,32,256]{2,1,0:T(8,128)(2,1)S(1)}, u32[]{:S(2)}, u32[]{:S(2)}) async-start(bf16[32,32,256]{2,1,0:T(8,128)(2,1)} %stack.8), calls=%async_computation | async-start | bytes 1048576 | tf_op jit(solution)/shard_map/while/body/eval_jaxpr/all_to_all | solution.py:10
  1350.4 1.4 copy-start
  1409.3 51.8 %all-to-all-start = ((bf16[32,32,256]{2,1,0:T(8,128)(2,1)}), bf16[32,32,256]{2,1,0:T(8,128)(2,1)S(1)}, u32[]{:S(2)}, u32[]{:S(2)}) async-start(bf16[32,32,256]{2,1,0:T(8,128)(2,1)} %stack.8), calls=%async_computation | async-start | bytes 1048576 | tf_op jit(solution)/shard_map/while/body/eval_jaxpr/all_to_all | solution.py:10
  1461.1 1.4 copy-start
  1519.9 51.8 %all-to-all-start = ((bf16[32,32,256]{2,1,0:T(8,128)(2,1)}), bf16[32,32,256]{2,1,0:T(8,128)(2,1)S(1)}, u32[]{:S(2)}, u32[]{:S(2)}) async-start(bf16[32,32,256]{2,1,0:T(8,128)(2,1)} %stack.8), calls=%async_computation | async-start | bytes 1048576 | tf_op jit(solution)/shard_map/while/body/eval_jaxpr/all_to_all | solution.py:10
  1571.7 1.4 copy-start
  1630.6 51.8 %all-to-all-start = ((bf16[32,32,256]{2,1,0:T(8,128)(2,1)}), bf16[32,32,256]{2,1,0:T(8,128)(2,1)S(1)}, u32[]{:S(2)}, u32[]{:S(2)}) async-start(bf16[32,32,256]{2,1,0:T(8,128)(2,1)} %stack.8), calls=%async_computation | async-start | bytes 1048576 | tf_op jit(solution)/shard_map/while/body/eval_jaxpr/all_to_all | solution.py:10
  1682.3 1.4 copy-start
  1741.2 51.8 %all-to-all-start = ((bf16[32,32,256]{2,1,0:T(8,128)(2,1)}), bf16[32,32,256]{2,1,0:T(8,128)(2,1)S(1)}, u32[]{:S(2)}, u32[]{:S(2)}) async-start(bf16[32,32,256]{2,1,0:T(8,128)(2,1)} %stack.8), calls=%async_computation | async-start | bytes 1048576 | tf_op jit(solution)/shard_map/while/body/eval_jaxpr/all_to_all | solution.py:10
  1793.0 1.4 copy-start
  (1 other events, 0.8 us)
